TPU v7x, 256 devices: a whole 4x4x8 slice. The times are simulated.
256 devices in a mesh: pipe: 4 (over z_lo, core), seq: 16 (over x, z_hi), head: 4 (over y).
Axes of the slice: x: 4, y: 4, z: 8 (z_hi: 4, z_lo: 2; z = z_hi * 2 + z_lo), core: 2. Of those that a mesh axis runs over, the one named last changes fastest.
Arguments:
- section_input: bfloat16 [4, 2048, 3, 2048], P('pipe', ('seq', 'head')), may hold values from -8 to 8
- grad_input: bfloat16 [4, 2048, 2048], P('pipe', ('seq', 'head')), may hold values from -6 to 6
- strided_blocks: int32 [16, 14], replicated, may hold values from 0 to 13, as said below
- strided_count: int32 [16], replicated, may hold values from 0 to 14, as said below
Outputs:
- attn_out: bfloat16 [4, 2048, 2048], P('pipe', ('seq', 'head'))
- grad_qkv: bfloat16 [4, 2048, 3, 2048], P('pipe', ('seq', 'head'))
Inputs may be any that keep to these rules, and one draw needn't show every extreme that they name: `strided_blocks`: row b holds in its first strided_count[b] entries distinct key blocks, each below b - 1; its other entries are 0 and unused. strided_count[b] is at most min(14, b - 1) for b >= 1 and 0 for b = 0; the last query block lists exactly 14.
All inputs are finite; a program needn't handle non-finite values.
Results may differ from a plain program's by a relative error of at most 0.0081.
Values may be sent and summed in bfloat16 or wider, within the bound.
A program may use at most 128 MiB of HBM per device.

v0:
```python
import math

import jax
import jax.numpy as jnp
from jax import lax
from jax.sharding import PartitionSpec as P

HD = 128
BLK = 128


def passed_along(x, axis, by):
    size = lax.axis_size(axis)
    return lax.ppermute(x, axis, [(i, (i + by) % size) for i in range(size)])


def slot_tables(block_ids, strided_blocks, strided_count):
    listed = strided_blocks[block_ids]
    list_width = listed.shape[1]
    slot_index = jnp.concatenate(
        [block_ids[:, None], jnp.maximum(block_ids - 1, 0)[:, None], listed], axis=1
    )
    first_valid = jnp.ones((block_ids.shape[0], 1), bool)
    second_valid = (block_ids >= 1)[:, None]
    listed_valid = jnp.arange(list_width)[None, :] < strided_count[block_ids][:, None]
    slot_valid = jnp.concatenate([first_valid, second_valid, listed_valid], axis=1)
    return (slot_index, slot_valid)


def body(section_input, grad_input, strided_blocks, strided_count):
    grad_cols = grad_input.reshape(grad_input.shape[0], grad_input.shape[1], 1, grad_input.shape[2])
    moved_input = passed_along(section_input, "pipe", 1)
    moved_grad = passed_along(grad_cols, "pipe", -1)
    heads_in, heads_grad = (
        lax.all_to_all(moved_input, "head", split_axis=3, concat_axis=1, tiled=True),
        lax.all_to_all(moved_grad, "head", split_axis=3, concat_axis=1, tiled=True),
    )
    qkv_here = heads_in[0]
    grad_here = heads_grad[0, :, 0]
    tok_rows = qkv_here.shape[0]
    local_width = qkv_here.shape[2]
    head_count = local_width // HD
    local_blocks = tok_rows // BLK
    att_scale = 1.0 / math.sqrt(HD)
    first_block = lax.axis_index("seq") * local_blocks
    block_ids = first_block + jnp.arange(local_blocks, dtype=jnp.int32)
    slot_index, slot_valid = slot_tables(block_ids, strided_blocks, strided_count)
    slot_count = slot_index.shape[1]
    gathered = lax.all_gather(qkv_here[:, 1:3], "seq", axis=0, tiled=True)
    total_blocks = gathered.shape[0] // BLK
    kv_blocks = gathered.reshape(total_blocks, BLK, 2, head_count, HD)[slot_index]
    keys_blk = kv_blocks[:, :, :, 0]
    values_blk = kv_blocks[:, :, :, 1]
    queries = qkv_here[:, 0].reshape(local_blocks, BLK, head_count, HD)
    grad_blk = grad_here.reshape(local_blocks, BLK, head_count, HD)
    causal = jnp.arange(BLK)[None, :] <= jnp.arange(BLK)[:, None]
    slot_first = jnp.arange(slot_count) == 0
    keep_mask = slot_valid[:, None, None, :, None] & (
        ~slot_first[None, None, None, :, None] | causal[None, None, :, None, :]
    )
    scores = (
        jnp.einsum("bqhd,bnkhd->bhqnk", queries, keys_blk, preferred_element_type=jnp.float32)
        * att_scale
    )
    row_max = jnp.max(jnp.where(keep_mask, scores, -jnp.inf), axis=(3, 4))
    row_total = jnp.sum(
        jnp.where(keep_mask, jnp.exp(scores - row_max[..., None, None]), 0.0), axis=(3, 4)
    )
    log_total = row_max + jnp.log(row_total)
    weights = jnp.where(keep_mask, jnp.exp(scores - log_total[..., None, None]), 0.0)
    weights_half = weights.astype(jnp.bfloat16)
    attended = jnp.einsum(
        "bhqnk,bnkhd->bqhd", weights_half, values_blk, preferred_element_type=jnp.float32
    )
    row_delta = jnp.sum(grad_blk.astype(jnp.float32) * attended, axis=-1).transpose(0, 2, 1)
    grad_w = jnp.einsum(
        "bqhd,bnkhd->bhqnk", grad_blk, values_blk, preferred_element_type=jnp.float32
    )
    grad_s = weights * (grad_w - row_delta[..., None, None])
    grad_half = grad_s.astype(jnp.bfloat16)
    grad_query = (
        jnp.einsum("bhqnk,bnkhd->bqhd", grad_half, keys_blk, preferred_element_type=jnp.float32)
        * att_scale
    )
    key_part = (
        jnp.einsum("bhqnk,bqhd->bnkhd", grad_half, queries, preferred_element_type=jnp.float32)
        * att_scale
    )
    value_part = jnp.einsum(
        "bhqnk,bqhd->bnkhd", weights_half, grad_blk, preferred_element_type=jnp.float32
    )
    parts = jnp.stack([key_part, value_part], axis=3).reshape(
        local_blocks * slot_count, BLK, 2, local_width
    )
    flat_index = slot_index.reshape(-1)
    flat_valid = slot_valid.reshape(-1).astype(jnp.float32)
    placed = jnp.zeros((total_blocks, BLK, 2, local_width), jnp.float32)
    placed = placed.at[flat_index].add(parts * flat_valid[:, None, None, None])
    placed_rows = placed.reshape(total_blocks * BLK, 2, local_width)
    key_sums = lax.psum_scatter(placed_rows, "seq", scatter_dimension=0, tiled=True)
    grad_keys = key_sums[:, 0].astype(jnp.bfloat16)
    grad_values = key_sums[:, 1].astype(jnp.bfloat16)
    grad_local = jnp.stack(
        [grad_query.reshape(tok_rows, local_width).astype(jnp.bfloat16), grad_keys, grad_values],
        axis=1,
    )[None]
    out_local = attended.astype(jnp.bfloat16).reshape(1, tok_rows, 1, local_width)
    out_rows, grad_rows = (
        lax.all_to_all(out_local, "head", split_axis=1, concat_axis=3, tiled=True),
        lax.all_to_all(grad_local, "head", split_axis=1, concat_axis=3, tiled=True),
    )
    return (out_rows.reshape(out_rows.shape[0], out_rows.shape[1], out_rows.shape[3]), grad_rows)


def solution(mesh):
    in_specs = (P("pipe", ("seq", "head"), None, None), P("pipe", ("seq", "head"), None), P(), P())
    out_specs = (P("pipe", ("seq", "head"), None), P("pipe", ("seq", "head"), None, None))
    return jax.shard_map(body, mesh=mesh, in_specs=in_specs, out_specs=out_specs, check_vma=False)
```

profile of v0, /device:TPU:1, one launch (start us, length us, event | category | flops | bytes accessed | tf_op | source)
XLA Modules:
  0.0 336.8 jit_solution(12367045121486279750)
XLA Ops:
  7.2 3.1 collective-permute-start
  10.3 5.0 %collective-permute-done = bf16[1,32,3,2048]{3,1,2,0:T(8,128)(2,1)S(1)} collective-permute-done((bf16[1,32,3,2048]{3,1,2,0:T(8,128)(2,1)}, bf16[1,32,3,2048]{3,1,2,0:T(8,128)(2,1)S(1)}, u32[]{:S(2)}, u32[]{:S(2)}) %collective-permute-start) | collective-permute-done | bytes 393248 | tf_op jit(solution)/shard_map/ppermute | solution.py:14
  15.4 1.3 copy.157
  16.7 1.6 reshape.456
  18.3 11.1 %all_to_all.63 = bf16[4,2,24576]{2,1,0:T(2,128)(2,1)S(1)} all-to-all(bf16[4,2,24576]{2,1,0:T(2,128)(2,1)S(1)} %reshape.456), channel_id=1, replica_groups=mesh['pipe'=4,'seq'=16,'head'=4] {'head'}, dimensions={0} | all-to-all | bytes 786432 | tf_op jit(solution)/shard_map/all_to_all | solution.py:35
  29.4 1.3 reshape.457
  30.8 1.2 copy.201
  32.0 0.1 copy.159
  32.0 0.7 slice.41
  32.8 2.1 collective-permute-start.1
  34.9 0.6 dynamic-slice.6
  35.6 0.6 iota_compare_fusion.1
  36.2 0.1 fusion.20
  36.3 0.2 or_and_fusion
  36.6 0.1 fusion.15
  36.6 2.0 collective-permute-done.1
  38.6 0.7 copy.169
  39.3 0.6 broadcast.147
  39.9 11.5 %reduce.5 = bf16[2048,32]{1,0:T(8,128)(2,1)S(1)} reduce(bf16[2048,1,1,32]{3,2,1,0:T(2,128)(2,1)S(1)} %bitcast.178, bf16[]{:T(256)} %broadcast.147), dimensions={1,2}, to_apply=%bitcast.151.reduce_sub_computation | reduce | bytes 262146
  51.4 1.2 reshape.460
  52.6 3.3 all-to-all-start.2
  56.0 0.2 reduce-scatter.2.cloned.1.call-start
  56.2 0.1 fusion.16
  56.3 4.8 %all-to-all-done.2 = bf16[4,2,8192]{2,1,0:T(2,128)(2,1)S(1)} async-done(((bf16[4,2,8192]{2,1,0:T(2,128)(2,1)}), bf16[4,2,8192]{2,1,0:T(2,128)(2,1)S(1)}, u32[]{:S(2)}, u32[]{:S(2)}) %all-to-all-start.2) | async-done | bytes 131104 | tf_op jit(solution)/shard_map/all_to_all | solution.py:36
  61.0 0.7 reshape.461
  61.7 0.5 copy.170
  62.3 0.1 reshape.431
  62.4 0.1 copy.173
  62.6 0.1 copy.200
  62.7 0.1 copy.163
  62.9 46.7 %all-gather.2.cloned.1.call-done = bf16[2048,2,512]{2,0,1:T(8,128)(2,1)} async-done(((bf16[128,2,512]{2,0,1:T(8,128)(2,1)}), bf16[2048,2,512]{2,0,1:T(8,128)(2,1)}) %all-gather.2.cloned.1.call-update) | async-done | bytes 4194320 | tf_op jit(solution)/shard_map/all_gather | solution.py:49
  109.5 7.0 %reshape.455 = bf16[16,128,2,4,128]{4,3,1,0,2:T(4,128)(2,1)} reshape(bf16[2048,2,512]{2,0,1:T(8,128)(2,1)} %all-gather.2.cloned.1.call-done) | data formatting | bytes 8388608 | tf_op jit(solution)/shard_map/reshape | solution.py:51
  116.5 5.3 %copy.161 = bf16[16,128,2,4,128]{4,1,3,2,0:T(8,128)(2,1)} copy(bf16[16,128,2,4,128]{4,3,1,0,2:T(4,128)(2,1)} %reshape.455) | data formatting | bytes 8388608 | tf_op jit(solution)/shard_map/reshape | solution.py:51
  121.8 5.2 %gather_fusion = bf16[16,128,2,4,128]{4,1,3,2,0:T(8,128)(2,1)} fusion(bf16[16,128,2,4,128]{4,1,3,2,0:T(8,128)(2,1)} %copy.161, s32[1024]{0:T(1024)S(1)} %pad_clamp_fusion), kind=kCustom, calls=%fused_computation | custom fusion | bytes 8388672 | tf_op jit(solution)/shard_map/gather | solution.py:51
  127.0 2.8 copy.217
  129.8 0.8 fusion.1
  130.6 0.9 fusion.4
  131.5 1.5 multiply_reduce_fusion
  132.9 1.1 convolution_bitcast_fusion
  134.0 1.4 fusion
  135.5 2.5 copy.181
  137.9 2.7 multiply_bitcast_fusion
  140.6 5.4 %copy.178 = f32[1,16,128,4,128]{2,4,3,1,0:T(8,128)} copy(f32[1,16,128,4,128]{4,2,1,3,0:T(8,128)} %multiply_bitcast_fusion) | data formatting | bytes 8388608 | tf_op jit(solution)/shard_map/mul | solution.py:86
  145.9 7.8 %maximum_multiply_fusion = f32[16,128,2,512]{1,3,0,2:T(8,128)} fusion(f32[16,128,1,512]{1,3,0,2:T(8,128)} %bitcast.169, f32[16,128,1,512]{1,3,0,2:T(8,128)} %bitcast.170, f32[16]{0:T(128)S(1)} %get-tuple-element.24), kind=kLoop, calls=%fused_computation.2 | loop fusion | flops 4194304 | bytes 16777280 | tf_op jit(solution)/shard_map/mul | solution.py:98
  153.8 9.3 %copy.182 = f32[16,128,2,512]{3,1,2,0:T(8,128)} copy(f32[16,128,2,512]{1,3,0,2:T(8,128)} %maximum_multiply_fusion) | data formatting | bytes 16777216 | tf_op jit(solution)/shard_map/mul | solution.py:98
  163.1 4.4 %broadcast_in_dim.56 = f32[16,128,2,512]{3,1,2,0:T(8,128)} broadcast(f32[]{:T(128)} %constant.10.clone.1), dimensions={} | broadcast | bytes 8388612 | tf_op jit(solution)/shard_map/broadcast_in_dim | solution.py:97
  167.4 16.4 %scatter_fusion = f32[16,128,2,512]{3,1,2,0:T(8,128)} fusion(f32[16,128,2,512]{3,1,2,0:T(8,128)} %broadcast_in_dim.56, s32[16]{0:T(128)S(1)} %fusion.16, f32[16,128,2,512]{3,1,2,0:T(8,128)} %copy.182), kind=kCustom, calls=%fused_computation.1 | custom fusion | flops 2097152 | bytes 25165888 | tf_op jit(solution)/shard_map/scatter-add | solution.py:98
  183.8 8.2 %copy.183 = f32[16,128,2,512]{3,1,0,2:T(8,128)} copy(f32[16,128,2,512]{3,1,2,0:T(8,128)} %scatter_fusion) | data formatting | bytes 16777216 | tf_op jit(solution)/shard_map/scatter-add | solution.py:98
  192.0 0.2 copy.167
  192.2 1.4 reduce.6
  193.6 0.7 reshape.458
  194.3 5.3 %all-to-all-start.1 = ((bf16[4,2,8192]{2,1,0:T(2,128)(2,1)}), bf16[4,2,8192]{2,1,0:T(2,128)(2,1)S(1)}, u32[]{:S(2)}, u32[]{:S(2)}) async-start(bf16[4,2,8192]{2,1,0:T(2,128)(2,1)} %reshape.458), calls=%async_computation.1 | async-start | bytes 262144 | tf_op jit(solution)/shard_map/all_to_all | solution.py:109
  199.7 2.4 fusion.14
  202.1 0.1 copy.184
  202.2 112.8 %reduce-scatter.2.cloned.1.call-done = f32[128,2,512]{2,0,1:T(8,128)} async-done(((f32[2048,2,512]{2,0,1:T(8,128)}), f32[128,2,512]{2,0,1:T(8,128)}) %reduce-scatter.2.cloned.1.call-update) | async-done | bytes 524304 | tf_op jit(solution)/shard_map/reduce_scatter | solution.py:100
  314.9 1.1 convert.5
  316.1 1.1 copy.185
  317.2 3.9 %all-to-all-start.3 = ((bf16[1,128,3,512]{3,2,0,1:T(4,128)(2,1)}), bf16[1,128,3,512]{3,2,0,1:T(4,128)(2,1)S(1)}, u32[]{:S(2)}, u32[]{:S(2)}) async-start(bf16[1,128,3,512]{3,2,0,1:T(4,128)(2,1)} %copy.185), calls=%async_computation.4 | async-start | bytes 1048576 | tf_op jit(solution)/shard_map/all_to_all | solution.py:110
  321.1 0.1 reshape.459
  321.3 0.1 copy.168
  321.4 0.7 reshape.387
  322.1 7.0 %all-to-all-done.3 = bf16[1,128,3,512]{3,2,0,1:T(4,128)(2,1)S(1)} async-done(((bf16[1,128,3,512]{3,2,0,1:T(4,128)(2,1)}), bf16[1,128,3,512]{3,2,0,1:T(4,128)(2,1)S(1)}, u32[]{:S(2)}, u32[]{:S(2)}) %all-to-all-start.3) | async-done | bytes 393248 | tf_op jit(solution)/shard_map/all_to_all | solution.py:110
  329.1 0.1 copy.186
  329.2 0.8 copy.212
  (25 shorter events, 0.3 us)
Async XLA Ops:
  7.2 28.4 %copy-start = (s32[16,14]{1,0:T(8,128)S(1)}, s32[16,14]{1,0:T(8,128)}, u32[]{:S(2)}) copy-start(s32[16,14]{1,0:T(8,128)} %param.6) | copy-start | bytes 2692
  7.2 102.3 %all-gather.2.cloned.1.call-start = ((), (), s32[]{:S(2)}) async-start(), calls=%async_computation.5 | async-start | bytes 4456448 | tf_op jit(solution)/shard_map/all_gather | solution.py:49
  7.2 8.1 %collective-permute-start = (bf16[1,32,3,2048]{3,1,2,0:T(8,128)(2,1)}, bf16[1,32,3,2048]{3,1,2,0:T(8,128)(2,1)S(1)}, u32[]{:S(2)}, u32[]{:S(2)}) collective-permute-start(bf16[1,32,3,2048]{3,1,2,0:T(8,128)(2,1)} %param.4), channel_id=1, source_target_pairs={{0,64},{64,128},{128,192},{192,0},{1,65},{65,129},{129,193},{193,1... | collective-permute-start | bytes 1179656 | tf_op jit(solution)/shard_map/ppermute | solution.py:14
  18.3 14.5 %copy-start.3 = (bf16[1,32,2048]{2,1,0:T(8,128)(2,1)S(1)}, bf16[1,32,2048]{2,1,0:T(8,128)(2,1)}, u32[]{:S(2)}) copy-start(bf16[1,32,2048]{2,1,0:T(8,128)(2,1)} %param.5) | copy-start | bytes 393220
  18.3 16.6 %copy-start.4 = (s32[16]{0:T(128)S(1)}, s32[16]{0:T(128)}, u32[]{:S(2)}) copy-start(s32[16]{0:T(128)} %param.7) | copy-start | bytes 196
  32.8 5.8 %collective-permute-start.1 = (bf16[1,32,1,2048]{3,1,2,0:T(8,128)(2,1)S(1)}, bf16[1,32,1,2048]{3,1,2,0:T(8,128)(2,1)S(1)}, u32[]{:S(2)}, u32[]{:S(2)}) collective-permute-start(bf16[1,32,1,2048]{3,1,2,0:T(8,128)(2,1)S(1)} %bitcast.193), channel_id=1, source_target_pairs={{0,192},{64,0},{128,64},{192,128},{1,193},{65,1},{129,65},{193,129... | collective-permute-start | bytes 393224 | tf_op jit(solution)/shard_map/ppermute | solution.py:14
  52.6 8.4 %all-to-all-start.2 = ((bf16[4,2,8192]{2,1,0:T(2,128)(2,1)}), bf16[4,2,8192]{2,1,0:T(2,128)(2,1)S(1)}, u32[]{:S(2)}, u32[]{:S(2)}) async-start(bf16[4,2,8192]{2,1,0:T(2,128)(2,1)} %reshape.460), calls=%async_computation.2 | async-start | bytes 262144 | tf_op jit(solution)/shard_map/all_to_all | solution.py:36
  56.0 259.0 %reduce-scatter.2.cloned.1.call-start = ((), (), s32[]{:S(2)}) async-start(), calls=%async_computation.6 | async-start | bytes 8912896 | tf_op jit(solution)/shard_map/reduce_scatter | solution.py:100
  129.8 4.3 %copy-start.2 = (bf16[16,128,2,4,128]{4,1,0,3,2:T(8,128)(2,1)}, bf16[16,128,2,4,128]{4,1,0,3,2:T(8,128)(2,1)S(1)}, u32[]{:S(2)}) copy-start(bf16[16,128,2,4,128]{4,1,0,3,2:T(8,128)(2,1)S(1)} %copy.217) | copy-start | bytes 12582916
  194.3 122.9 %all-to-all-start.1 = ((bf16[4,2,8192]{2,1,0:T(2,128)(2,1)}), bf16[4,2,8192]{2,1,0:T(2,128)(2,1)S(1)}, u32[]{:S(2)}, u32[]{:S(2)}) async-start(bf16[4,2,8192]{2,1,0:T(2,128)(2,1)} %reshape.458), calls=%async_computation.1 | async-start | bytes 262144 | tf_op jit(solution)/shard_map/all_to_all | solution.py:109
  199.7 130.3 %copy-start.1 = (s32[16,14]{1,0:T(8,128)S(1)}, s32[16,14]{1,0:T(8,128)}, u32[]{:S(2)}) copy-start(s32[16,14]{1,0:T(8,128)} %param.6) | copy-start | bytes 2692
  317.2 11.9 %all-to-all-start.3 = ((bf16[1,128,3,512]{3,2,0,1:T(4,128)(2,1)}), bf16[1,128,3,512]{3,2,0,1:T(4,128)(2,1)S(1)}, u32[]{:S(2)}, u32[]{:S(2)}) async-start(bf16[1,128,3,512]{3,2,0,1:T(4,128)(2,1)} %copy.185), calls=%async_computation.4 | async-start | bytes 1048576 | tf_op jit(solution)/shard_map/all_to_all | solution.py:110
Sparse Core Ops, SparseCore 0:
  32.9 76.5 all-gather.1
  192.1 122.7 reduce-scatter.1
where the time goes:
time: 339 us; the launch traced here: 337 us
  waiting for transfers between devices  178 us (53%)
  local copies, waits for them, and re-layouts  65 us (19%)
  other arithmetic  40.3 us (12%)
  starting transfers between devices  18 us (5%)
  between operations  14.3 us (4%)
  blocking collectives  11.1 us (3%)
  matrix products  9.79 us (3%)
    reduce_scatter x1, waiting for transfers between devices, body(): lax.psum_scatter(placed_rows, 'seq', scatter_dimension=0, tiled=True)  113 us
    all_gather x1, waiting for transfers between devices, body(): gathered = lax.all_gather(qkv_here[:, 1:3], 'seq', axis=0, tiled=True)  46.7 us
    scatter-add x1, other arithmetic, body(): placed = placed.at[flat_index].add(parts * flat_valid[:, None, None, None])  16.4 us
    unnamed x2, other arithmetic  12.9 us
    reshape x2, local copies, waits for them, and re-layouts, body(): gathered.reshape(total_blocks, BLK, 2, head_count, HD)[slot_index]  12.3 us
    all_to_all x1, blocking collectives, body(): lax.all_to_all(moved_input, 'head', split_axis=3, concat_axis=1, tiled=True)  11.1 us
    mul x1, local copies, waits for them, and re-layouts, body(): placed = placed.at[flat_index].add(parts * flat_valid[:, None, None, None])  9.28 us
    scatter-add x1, local copies, waits for them, and re-layouts, body(): placed = placed.at[flat_index].add(parts * flat_valid[:, None, None, None])  8.18 us
  transfers between devices with their start and end apart: 7, of which 6 were waited for; matrix products, arithmetic and copies ran while one was open for 8% of the time, Pallas kernels for 0%

commit v1 on v0

v1 whole, which is shorter than its diff:
```python
import math

import jax
import jax.numpy as jnp
from jax import lax
from jax.experimental import pallas as pl
from jax.experimental.pallas import tpu as pltpu
from jax.sharding import PartitionSpec as P

HD = 128
BLK = 128
TILE = 256
SEQ = 2048
NB = SEQ // BLK
NT = SEQ // TILE
N_PIPE = 4
N_SEQ = 16
N_HEAD = 4
HEADS = 16
ROWS = 32
SMAX = 14
SCALE = 1.0 / math.sqrt(HD)
SCALE2 = math.log2(math.e) / math.sqrt(HD)
NEG = -1e30
F32 = jnp.float32
BF16 = jnp.bfloat16
MESH = pl.DeviceIdType.MESH


def dot_nt(a, b):
    return lax.dot_general(a, b, (((1,), (1,)), ((), ())), preferred_element_type=F32)


def dot_nn(a, b):
    return lax.dot_general(a, b, (((1,), (0,)), ((), ())), preferred_element_type=F32)


def owner_of(section, head):
    x, y = head // 4, head % 4
    z_lo = 1 - section // 2
    z_hi = (x + (section % 2) * 2 + section // 2) % 4
    return (2 * z_lo + section % 2, x * 4 + z_hi, y)


def owned_by(pipe, seq, y):
    x, z_hi = seq // 4, seq % 4
    half = 1 - pipe // 2
    section = 2 * half + pipe % 2
    is_owner = z_hi == (x + (pipe % 2) * 2 + half) % 4
    return is_owner, section, x * 4 + y


def kept_words(blocks_ref, count_ref, words_ref):
    def one(b, _):
        word = jnp.where(b > 0, jnp.left_shift(1, jnp.maximum(b - 1, 0)), 0)
        for t in range(SMAX):
            bit = jnp.left_shift(1, blocks_ref[b, t])
            word = word | jnp.where(t < count_ref[b], bit, 0)
        words_ref[b] = word
        return 0

    lax.fori_loop(0, NB, one, 0)


def transposed(x_ref, kt_ref, vt_ref):
    def one(j, _):
        rows = pl.ds(pl.multiple_of(j * TILE, TILE), TILE)
        kt_ref[j] = x_ref[1, rows, :].T
        vt_ref[j] = x_ref[2, rows, :].T
        return 0

    lax.fori_loop(0, NT, one, 0)


def query_tile(b, bias, before_grad, x_ref, g_ref, kt_ref, vt_ref, s_ref, e_ref, dk_ref, dv_ref, o_ref, d_ref):
    rows_q = slice(b * TILE, (b + 1) * TILE)
    q = x_ref[0, rows_q, :]
    lane = lax.broadcasted_iota(jnp.int32, (1, TILE), 1)
    top = jnp.full((8, TILE), NEG, F32)
    for j in range(b + 1):
        s = dot_nt(x_ref[1, j * TILE : (j + 1) * TILE, :], q) * SCALE2
        if j == b:
            key = lax.broadcasted_iota(jnp.int32, (TILE, TILE), 0)
            query = lax.broadcasted_iota(jnp.int32, (TILE, TILE), 1)
            s = jnp.where(key <= query, s, NEG)
        else:
            halves = []
            for half in range(2):
                row = jnp.where(lane < BLK, bias(2 * b, 2 * j + half), bias(2 * b + 1, 2 * j + half))
                halves.append(s[half * BLK : (half + 1) * BLK] + row)
            s = jnp.concatenate(halves, axis=0)
        s_ref[j] = s
        top = jnp.maximum(top, jnp.max(s.reshape(TILE // 8, 8, TILE), axis=0))
    top = jnp.max(top, axis=0, keepdims=True)
    total = jnp.zeros((8, TILE), F32)
    out = jnp.zeros((HD, TILE), F32)
    for j in range(b + 1):
        e = jnp.exp2(s_ref[j] - top)
        total = total + jnp.sum(e.reshape(TILE // 8, 8, TILE), axis=0)
        e = e.astype(BF16)
        e_ref[j] = e
        out = out + dot_nn(vt_ref[j], e)
    inverse = 1.0 / jnp.sum(total, axis=0, keepdims=True)
    out = out * inverse
    before_grad()
    g = g_ref[rows_q, :]
    delta = jnp.sum(out * g.astype(F32).T, axis=0, keepdims=True)
    o_ref[rows_q, :] = out.T.astype(BF16)
    dq = jnp.zeros((HD, TILE), F32)
    for j in range(b + 1):
        rows_k = slice(j * TILE, (j + 1) * TILE)
        p = e_ref[j].astype(F32) * inverse
        dp = dot_nt(x_ref[2, rows_k, :], g)
        ds = (p * (dp - delta)).astype(BF16)
        dv = dot_nn(p.astype(BF16), g)
        dk = dot_nn(ds, q)
        if b == NT - 1:
            dv_ref[rows_k, :] = dv
            dk_ref[rows_k, :] = dk
        else:
            dv_ref[rows_k, :] += dv
            dk_ref[rows_k, :] += dk
        dq = dq + dot_nn(kt_ref[j], ds)
    d_ref[0, rows_q, :] = (dq.T * SCALE).astype(BF16)
    d_ref[1, rows_q, :] = (dk_ref[rows_q, :] * SCALE).astype(BF16)
    d_ref[2, rows_q, :] = dv_ref[rows_q, :].astype(BF16)


def kernel(
    blocks_ref, count_ref, x_hbm, g_hbm, o_hbm, d_hbm,
    x_ref, g_ref, o_ref, d_ref, kt_ref, vt_ref, s_ref, e_ref, dk_ref, dv_ref, words_ref,
    send_x, send_g, send_o, send_d, recv_x, recv_g, recv_o, recv_d,
):
    pipe, seq, y = lax.axis_index("pipe"), lax.axis_index("seq"), lax.axis_index("head")
    is_owner, section, head = owned_by(pipe, seq, y)
    first_row = pl.multiple_of(seq * BLK + y * ROWS, ROWS)
    mine = pl.ds(first_row, ROWS)

    def send_x_to(i):
        h = (i + seq + 4 * y) % HEADS
        lanes = pl.ds(pl.multiple_of(h * HD, HD), HD)
        return pltpu.make_async_remote_copy(
            src_ref=x_hbm.at[:, :, lanes], dst_ref=x_ref.at[:, mine, :],
            send_sem=send_x, recv_sem=recv_x,
            device_id=owner_of((pipe + 1) % N_PIPE, h), device_id_type=MESH,
        )

    def send_g_to(i):
        h = (i + seq + 4 * y) % HEADS
        lanes = pl.ds(pl.multiple_of(h * HD, HD), HD)
        return pltpu.make_async_remote_copy(
            src_ref=g_hbm.at[:, lanes], dst_ref=g_ref.at[mine, :],
            send_sem=send_g, recv_sem=recv_g,
            device_id=owner_of((pipe + 3) % N_PIPE, h), device_id_type=MESH,
        )

    @pl.loop(0, HEADS)
    def _(i):
        send_x_to(i).start()

    @pl.loop(0, HEADS)
    def _(i):
        send_g_to(i).start()

    def wait_all(ref, sem):
        pltpu.make_async_copy(ref, ref, sem).wait()

    @pl.when(is_owner)
    def _():
        lanes = pl.ds(pl.multiple_of(head * HD, HD), HD)
        kept_words(blocks_ref, count_ref, words_ref)

        def bias(b, j):
            return jnp.where((words_ref[b] & (1 << j)) != 0, 0.0, NEG)

        wait_all(x_ref, recv_x)
        transposed(x_ref, kt_ref, vt_ref)
        for b in range(NT - 1, -1, -1):
            query_tile(
                b, bias, (lambda: wait_all(g_ref, recv_g)) if b == NT - 1 else (lambda: None),
                x_ref, g_ref, kt_ref, vt_ref, s_ref, e_ref, dk_ref, dv_ref, o_ref, d_ref,
            )

            @pl.loop(0, 8)
            def _(i):
                to_seq, to_y = 2 * b + i // 4, i % 4
                rows = pl.ds(pl.multiple_of(to_seq * BLK + to_y * ROWS, ROWS), ROWS)
                pltpu.make_async_remote_copy(
                    src_ref=o_ref.at[rows, :], dst_ref=o_hbm.at[:, lanes],
                    send_sem=send_o, recv_sem=recv_o,
                    device_id=(section, to_seq, to_y), device_id_type=MESH,
                ).start()
                pltpu.make_async_remote_copy(
                    src_ref=d_ref.at[:, rows, :], dst_ref=d_hbm.at[:, :, lanes],
                    send_sem=send_d, recv_sem=recv_d,
                    device_id=(section, to_seq, to_y), device_id_type=MESH,
                ).start()

        wait_all(o_ref, send_o)
        wait_all(d_ref, send_d)

    wait_all(x_hbm, send_x)
    wait_all(g_hbm, send_g)
    wait_all(o_hbm, recv_o)
    wait_all(d_hbm, recv_d)


def body(section_input, grad_input, strided_blocks, strided_count):
    x = jnp.transpose(section_input[0], (1, 0, 2))
    g = grad_input[0]
    hbm = pl.BlockSpec(memory_space=pl.ANY)
    smem = pl.BlockSpec(memory_space=pltpu.SMEM)
    width = HEADS * HD
    out, grads = pl.pallas_call(
        kernel,
        out_shape=(
            jax.ShapeDtypeStruct((ROWS, width), BF16),
            jax.ShapeDtypeStruct((3, ROWS, width), BF16),
        ),
        in_specs=[smem, smem, hbm, hbm],
        out_specs=(hbm, hbm),
        scratch_shapes=[
            pltpu.VMEM((3, SEQ, HD), BF16),
            pltpu.VMEM((SEQ, HD), BF16),
            pltpu.VMEM((SEQ, HD), BF16),
            pltpu.VMEM((3, SEQ, HD), BF16),
            pltpu.VMEM((NT, HD, TILE), BF16),
            pltpu.VMEM((NT, HD, TILE), BF16),
            pltpu.VMEM((NT, TILE, TILE), F32),
            pltpu.VMEM((NT, TILE, TILE), BF16),
            pltpu.VMEM((SEQ, HD), F32),
            pltpu.VMEM((SEQ, HD), F32),
            pltpu.SMEM((NB,), jnp.int32),
        ]
        + [pltpu.SemaphoreType.DMA] * 8,
        compiler_params=pltpu.CompilerParams(has_side_effects=True, vmem_limit_bytes=40 << 20),
    )(strided_blocks, strided_count, x, g)
    return out[None], jnp.transpose(grads, (1, 0, 2))[None]


def solution(mesh):
    in_specs = (P("pipe", ("seq", "head"), None, None), P("pipe", ("seq", "head"), None), P(), P())
    out_specs = (P("pipe", ("seq", "head"), None), P("pipe", ("seq", "head"), None, None))
    return jax.shard_map(body, mesh=mesh, in_specs=in_specs, out_specs=out_specs, check_vma=False)
```

time: 339 us -> 65.9 us (0.19)
  waiting for transfers between devices: 178 us -> 0 us
  Pallas kernels: 0 us -> 60.4 us
  local copies, waits for them, and re-layouts: 65 us -> 4.65 us
  other arithmetic: 40.3 us -> 0 us
  starting transfers between devices: 18 us -> 0 us
  between operations: 14.3 us -> 0.65 us
  blocking collectives: 11.1 us -> 0 us
  matrix products: 9.79 us -> 0 us
    reduce_scatter x1 -> x0, waiting for transfers between devices: 113 us -> none  [body(): lax.psum_scatter(placed_rows, 'seq', scatter_dimension=0, tiled=True)]
    pallas_call x0 -> x1, Pallas kernels: none -> 60.4 us  [body(): pl.pallas_call(kernel, out_shape=(jax.ShapeDtypeStruct((ROWS, width), BF1...]
    all_gather x1 -> x0, waiting for transfers between devices: 46.7 us -> none  [body(): gathered = lax.all_gather(qkv_here[:, 1:3], 'seq', axis=0, tiled=True)]
    scatter-add x1 -> x0, other arithmetic: 16.4 us -> none  [body(): placed = placed.at[flat_index].add(parts * flat_valid[:, None, None, None])]
    mul x2 -> x0, local copies, waits for them, and re-layouts: 14.6 us -> none  [the longest x1 9.28 us: body(): placed = placed.at[flat_index].add(parts * flat_valid[:, None, None, None])]
    reshape x4 -> x0, local copies, waits for them, and re-layouts: 13.2 us -> none  [the longest x2 12.3 us: body(): gathered.reshape(total_blocks, BLK, 2, head_count, HD)[slot_index]]
    unnamed x2 -> x0, other arithmetic: 12.9 us -> none
    all_to_all x3 -> x0, starting transfers between devices: 12.5 us -> none  [the longest x1 5.31 us: body(): lax.all_to_all(out_local, 'head', split_axis=1, concat_axis=3, tiled=True)]
  transfers between devices with their start and end apart: 7 -> 0, of which waited for: 6 -> 0; matrix products, arithmetic and copies ran while one was open for 8% -> 0% of each run, Pallas kernels for 0% -> 0%
where the time goes in v1:
time: 65.9 us; the launch traced here: 65.7 us
  Pallas kernels  60.4 us (92%)
  local copies, waits for them, and re-layouts  4.65 us (7%)
    pallas_call x1, Pallas kernels, body(): pl.pallas_call(kernel, out_shape=(jax.ShapeDtypeStruct((ROWS, width), BF1...  60.4 us
    unnamed x10, local copies, waits for them, and re-layouts  4.65 us

profile of v1, /device:TPU:1, one launch (start us, length us, event | category | flops | bytes accessed | tf_op | source)
XLA Modules:
  0.0 65.7 jit_solution(3176165743616411260)
XLA Ops:
  0.6 0.0 copy-start.3
  0.6 0.6 copy-done.3
  1.3 0.0 copy-start
  1.3 1.0 %copy-done = bf16[1,32,3,2048]{3,1,2,0:T(8,128)(2,1)S(1)} copy-done((bf16[1,32,3,2048]{3,1,2,0:T(8,128)(2,1)S(1)}, bf16[1,32,3,2048]{3,1,2,0:T(8,128)(2,1)}, u32[]{:S(2)}) %copy-start) | copy-done | bytes 393240
  2.3 0.0 copy-start.1
  2.3 0.9 %copy-done.1 = bf16[1,32,2048]{2,1,0:T(8,128)(2,1)S(1)} copy-done((bf16[1,32,2048]{2,1,0:T(8,128)(2,1)S(1)}, bf16[1,32,2048]{2,1,0:T(8,128)(2,1)}, u32[]{:S(2)}) %copy-start.1) | copy-done | bytes 131096
  3.2 0.0 copy-start.2
  3.2 0.7 %copy-done.2 = s32[16,14]{1,0:T(8,128)S(1)} copy-done((s32[16,14]{1,0:T(8,128)S(1)}, s32[16,14]{1,0:T(8,128)}, u32[]{:S(2)}) %copy-start.2) | copy-done | bytes 920
  3.9 60.4 %shard_map.59 = (bf16[32,2048]{1,0:T(8,128)(2,1)S(1)}, bf16[3,32,2048]{2,1,0:T(8,128)(2,1)S(1)}) custom-call(s32[16,14]{1,0:T(8,128)S(1)} %copy-done.2, s32[16]{0:T(128)S(1)} %copy-done.3, bf16[3,32,2048]{2,1,0:T(8,128)(2,1)S(1)} %bitcast.8, bf16[32,2048]{1,0:T(8,128)(2,1)S(1)} %bitcast.10), custom_call_target="tpu_custom_call" | custom-call | tf_op jit(solution)/shard_map/pallas_call | solution.py:214
  64.3 0.7 %copy.8 = bf16[1,32,2048]{2,1,0:T(8,128)(2,1)} copy(bf16[1,32,2048]{2,1,0:T(8,128)(2,1)S(1)} %bitcast.11) | data formatting | bytes 262144
  64.9 0.7 %copy.9 = bf16[1,32,3,2048]{3,1,2,0:T(8,128)(2,1)} copy(bf16[1,32,3,2048]{3,1,2,0:T(8,128)(2,1)S(1)} %bitcast.9) | data formatting | bytes 786432
Async XLA Ops:
  0.6 0.7 copy-start.3
  1.3 1.0 %copy-start = (bf16[1,32,3,2048]{3,1,2,0:T(8,128)(2,1)S(1)}, bf16[1,32,3,2048]{3,1,2,0:T(8,128)(2,1)}, u32[]{:S(2)}) copy-start(bf16[1,32,3,2048]{3,1,2,0:T(8,128)(2,1)} %param.4) | copy-start | bytes 1179652
  2.3 0.9 %copy-start.1 = (bf16[1,32,2048]{2,1,0:T(8,128)(2,1)S(1)}, bf16[1,32,2048]{2,1,0:T(8,128)(2,1)}, u32[]{:S(2)}) copy-start(bf16[1,32,2048]{2,1,0:T(8,128)(2,1)} %param.5) | copy-start | bytes 393220
  3.2 0.7 %copy-start.2 = (s32[16,14]{1,0:T(8,128)S(1)}, s32[16,14]{1,0:T(8,128)}, u32[]{:S(2)}) copy-start(s32[16,14]{1,0:T(8,128)} %blocks_ref.1) | copy-start | bytes 2692

commit v2 on v1

v2 whole, which is shorter than its diff:
```python
import math

import jax
import jax.numpy as jnp
from jax import lax
from jax.experimental import pallas as pl
from jax.experimental.pallas import tpu as pltpu
from jax.sharding import PartitionSpec as P

HD = 128
BLK = 128
TILE = 256
SEQ = 2048
NB = SEQ // BLK
NT = SEQ // TILE
N_PIPE = 4
N_SEQ = 16
N_HEAD = 4
HEADS = 16
ROWS = 32
SMAX = 14
SCALE = 1.0 / math.sqrt(HD)
SCALE2 = math.log2(math.e) / math.sqrt(HD)
NEG = -1e30
VMEM_LIMIT = 40 * 1024 * 1024
F32 = jnp.float32
BF16 = jnp.bfloat16
MESH = pl.DeviceIdType.MESH


def dot_nt(a, b):
    return lax.dot_general(a, b, (((1,), (1,)), ((), ())), preferred_element_type=F32)


def dot_nn(a, b):
    return lax.dot_general(a, b, (((1,), (0,)), ((), ())), preferred_element_type=F32)


def owner_of(section, head):
    x, y = head // 4, head % 4
    z_lo = 1 - section // 2
    z_hi = (x + (section % 2) * 2 + section // 2) % 4
    return (2 * z_lo + section % 2, x * 4 + z_hi, y)


def owned_by(pipe, seq, y):
    x, z_hi = seq // 4, seq % 4
    half = 1 - pipe // 2
    section = 2 * half + pipe % 2
    is_owner = z_hi == (x + (pipe % 2) * 2 + half) % 4
    return is_owner, section, x * 4 + y


def kept_words(blocks_ref, count_ref, words_ref):
    def one(b, _):
        word = jnp.where(b > 0, jnp.left_shift(1, jnp.maximum(b - 1, 0)), 0)
        for t in range(SMAX):
            bit = jnp.left_shift(1, blocks_ref[b, t])
            word = word | jnp.where(t < count_ref[b], bit, 0)
        words_ref[b] = word
        return 0

    lax.fori_loop(0, NB, one, 0)


def transposed(x_ref, kt_ref, vt_ref):
    def one(j, _):
        rows = pl.ds(pl.multiple_of(j * TILE, TILE), TILE)
        kt_ref[j] = x_ref[1, rows, :].T
        vt_ref[j] = x_ref[2, rows, :].T
        return 0

    lax.fori_loop(0, NT, one, 0)


def query_tile(b, bias, before_grad, x_ref, g_ref, kt_ref, vt_ref, s_ref, e_ref, dk_ref, dv_ref, r_ref):
    rows_q = slice(b * TILE, (b + 1) * TILE)
    q = x_ref[0, rows_q, :]
    lane = lax.broadcasted_iota(jnp.int32, (1, TILE), 1)
    top = jnp.full((8, TILE), NEG, F32)
    for j in range(b + 1):
        s = dot_nt(x_ref[1, j * TILE : (j + 1) * TILE, :], q) * SCALE2
        if j == b:
            key = lax.broadcasted_iota(jnp.int32, (TILE, TILE), 0)
            query = lax.broadcasted_iota(jnp.int32, (TILE, TILE), 1)
            s = jnp.where(key <= query, s, NEG)
        else:
            halves = []
            for half in range(2):
                row = jnp.where(lane < BLK, bias(2 * b, 2 * j + half), bias(2 * b + 1, 2 * j + half))
                halves.append(s[half * BLK : (half + 1) * BLK] + row)
            s = jnp.concatenate(halves, axis=0)
        s_ref[j] = s
        top = jnp.maximum(top, jnp.max(s.reshape(TILE // 8, 8, TILE), axis=0))
    top = jnp.max(top, axis=0, keepdims=True)
    total = jnp.zeros((8, TILE), F32)
    out = jnp.zeros((HD, TILE), F32)
    for j in range(b + 1):
        e = jnp.exp2(s_ref[j] - top)
        total = total + jnp.sum(e.reshape(TILE // 8, 8, TILE), axis=0)
        e = e.astype(BF16)
        e_ref[j] = e
        out = out + dot_nn(vt_ref[j], e)
    inverse = 1.0 / jnp.sum(total, axis=0, keepdims=True)
    out = out * inverse
    before_grad()
    g = g_ref[rows_q, :]
    delta = jnp.sum(out * g.astype(F32).T, axis=0, keepdims=True)
    r_ref[0, rows_q, :] = out.T.astype(BF16)
    dq = jnp.zeros((HD, TILE), F32)
    for j in range(b + 1):
        rows_k = slice(j * TILE, (j + 1) * TILE)
        p = e_ref[j].astype(F32) * inverse
        dp = dot_nt(x_ref[2, rows_k, :], g)
        ds = (p * (dp - delta)).astype(BF16)
        dv = dot_nn(p.astype(BF16), g)
        dk = dot_nn(ds, q)
        if b == NT - 1:
            dv_ref[rows_k, :] = dv
            dk_ref[rows_k, :] = dk
        else:
            dv_ref[rows_k, :] += dv
            dk_ref[rows_k, :] += dk
        dq = dq + dot_nn(kt_ref[j], ds)
    r_ref[1, rows_q, :] = (dq.T * SCALE).astype(BF16)
    r_ref[2, rows_q, :] = (dk_ref[rows_q, :] * SCALE).astype(BF16)
    r_ref[3, rows_q, :] = dv_ref[rows_q, :].astype(BF16)


def kernel(
    blocks_ref, count_ref, x_hbm, g_hbm, r_out,
    x_ref, g_ref, r_ref, kt_ref, vt_ref, s_ref, e_ref, dk_ref, dv_ref, words_ref,
    send_x, send_g, send_r, recv_kv, recv_q, recv_g, recv_r,
):
    pipe, seq, y = lax.axis_index("pipe"), lax.axis_index("seq"), lax.axis_index("head")
    is_owner, section, head = owned_by(pipe, seq, y)
    x, z_hi = seq // 4, seq % 4
    order = (2, 1, 3, 0)
    xs, zs, ys = ([(at + k) % 4 for k in order] for at in (x, z_hi, y))
    after, before = (pipe + 1) % N_PIPE, (pipe + 3) % N_PIPE

    barrier = pltpu.get_barrier_semaphore()

    def ring(device):
        pl.semaphore_signal(barrier, inc=1, device_id=device, device_id_type=MESH)

    def owners(of):
        z_lo, shift = 1 - of // 2, (of % 2) * 2 + of // 2
        for to_x in xs:
            to_seq = to_x * 4 + (to_x + shift) % 4
            for to_y in ys:
                lanes = pl.ds(pl.multiple_of(to_x * (4 * HD) + to_y * HD, HD), HD)
                yield lanes, (2 * z_lo + of % 2, to_seq, to_y)

    @pl.when(is_owner)
    def _():
        for to_z in zs:
            for to_x in xs:
                to_seq = to_x * 4 + to_z
                for to_y in ys:
                    ring(((section + 1) % N_PIPE, to_seq, to_y))
                    ring(((section + 3) % N_PIPE, to_seq, to_y))

    for _, device in owners(pipe):
        ring(device)
    pl.semaphore_wait(barrier, 32 + 64 * is_owner.astype(jnp.int32))

    mine = pl.ds(pl.multiple_of(seq * BLK + y * ROWS, ROWS), ROWS)

    def pass_on(src_ref, dst_ref, send_sem, recv_sem, device):
        pltpu.make_async_remote_copy(
            src_ref=src_ref, dst_ref=dst_ref, send_sem=send_sem, recv_sem=recv_sem,
            device_id=device, device_id_type=MESH,
        ).start()

    for lanes, device in owners(after):
        pass_on(x_hbm.at[1:3, :, lanes], x_ref.at[1:3, mine, :], send_x, recv_kv, device)
    for lanes, device in owners(after):
        pass_on(x_hbm.at[0, :, lanes], x_ref.at[0, mine, :], send_x, recv_q, device)
    for lanes, device in owners(before):
        pass_on(g_hbm.at[:, lanes], g_ref.at[mine, :], send_g, recv_g, device)

    def wait_all(ref, sem):
        pltpu.make_async_copy(ref, ref, sem).wait()

    @pl.when(is_owner)
    def _():
        my_lanes = pl.ds(pl.multiple_of(head * HD, HD), HD)
        kept_words(blocks_ref, count_ref, words_ref)

        def bias(b, j):
            return jnp.where((words_ref[b] & (1 << j)) != 0, 0.0, NEG)

        wait_all(x_ref.at[1:3], recv_kv)
        transposed(x_ref, kt_ref, vt_ref)
        wait_all(x_ref.at[0], recv_q)
        for b in range(NT - 1, -1, -1):
            query_tile(
                b, bias, (lambda: wait_all(g_ref, recv_g)) if b == NT - 1 else (lambda: None),
                x_ref, g_ref, kt_ref, vt_ref, s_ref, e_ref, dk_ref, dv_ref, r_ref,
            )
            for to_y in ys:
                for to_seq in (2 * b, 2 * b + 1):
                    rows = pl.ds(pl.multiple_of(to_seq * BLK + to_y * ROWS, ROWS), ROWS)
                    pass_on(
                        r_ref.at[:, rows, :], r_out.at[:, :, my_lanes], send_r, recv_r,
                        (section, to_seq, to_y),
                    )
        wait_all(r_ref, send_r)

    wait_all(x_hbm, send_x)
    wait_all(g_hbm, send_g)
    wait_all(r_out, recv_r)


def body(section_input, grad_input, strided_blocks, strided_count):
    x = jnp.transpose(section_input[0], (1, 0, 2))
    g = pltpu.with_memory_space_constraint(grad_input[0], pltpu.HBM)
    x = pltpu.with_memory_space_constraint(x, pltpu.HBM)
    hbm = pl.BlockSpec(memory_space=pl.ANY)
    smem = pl.BlockSpec(memory_space=pltpu.SMEM)
    width = HEADS * HD
    result = pl.pallas_call(
        kernel,
        out_shape=jax.ShapeDtypeStruct((4, ROWS, width), BF16),
        in_specs=[smem, smem, hbm, hbm],
        out_specs=hbm,
        scratch_shapes=[
            pltpu.VMEM((3, SEQ, HD), BF16),
            pltpu.VMEM((SEQ, HD), BF16),
            pltpu.VMEM((4, SEQ, HD), BF16),
            pltpu.VMEM((NT, HD, TILE), BF16),
            pltpu.VMEM((NT, HD, TILE), BF16),
            pltpu.VMEM((NT, TILE, TILE), F32),
            pltpu.VMEM((NT, TILE, TILE), BF16),
            pltpu.VMEM((SEQ, HD), F32),
            pltpu.VMEM((SEQ, HD), F32),
            pltpu.SMEM((NB,), jnp.int32),
        ]
        + [pltpu.SemaphoreType.DMA] * 7,
        compiler_params=pltpu.CompilerParams(
            collective_id=0, has_side_effects=True, vmem_limit_bytes=VMEM_LIMIT
        ),
    )(strided_blocks, strided_count, x, g)
    return result[:1], jnp.transpose(result[1:], (1, 0, 2))[None]


def solution(mesh):
    in_specs = (P("pipe", ("seq", "head"), None, None), P("pipe", ("seq", "head"), None), P(), P())
    out_specs = (P("pipe", ("seq", "head"), None), P("pipe", ("seq", "head"), None, None))
    return jax.shard_map(body, mesh=mesh, in_specs=in_specs, out_specs=out_specs, check_vma=False)
```

time: 65.9 us -> 57.4 us (0.87)
  Pallas kernels: 60.4 us -> 53.8 us
  local copies, waits for them, and re-layouts: 4.65 us -> 2.78 us
    pallas_call x1, Pallas kernels: 60.4 us -> 53.8 us  [body(): pl.pallas_call(kernel, out_shape=jax.ShapeDtypeStruct((4, ROWS, width), B...]
    unnamed x10 -> x4, local copies, waits for them, and re-layouts: 4.65 us -> 1.34 us
    broadcast_in_dim x0 -> x1, local copies, waits for them, and re-layouts: none -> 0.77 us  [body(): return (result[:1], jnp.transpose(result[1:], (1, 0, 2))[None])]
    slice x0 -> x1, local copies, waits for them, and re-layouts: none -> 0.66 us  [body(): return (result[:1], jnp.transpose(result[1:], (1, 0, 2))[None])]
where the time goes in v2:
time: 57.4 us; the launch traced here: 57.3 us
  Pallas kernels  53.8 us (94%)
  local copies, waits for them, and re-layouts  2.78 us (5%)
  between operations  0.65 us (1%)
    pallas_call x1, Pallas kernels, body(): pl.pallas_call(kernel, out_shape=jax.ShapeDtypeStruct((4, ROWS, width), B...  53.8 us
    unnamed x4, local copies, waits for them, and re-layouts  1.34 us

profile of v2, /device:TPU:1, one launch (start us, length us, event | category | flops | bytes accessed | tf_op | source)
XLA Modules:
  0.0 57.3 jit_solution(8396943026587891805)
XLA Ops:
  0.6 0.0 copy-start.1
  0.6 0.6 %copy-done.1 = s32[16]{0:T(128)S(1)} copy-done((s32[16]{0:T(128)S(1)}, s32[16]{0:T(128)}, u32[]{:S(2)}) %copy-start.1) | copy-done | bytes 88
  1.3 0.0 copy-start
  1.3 0.7 %copy-done = s32[16,14]{1,0:T(8,128)S(1)} copy-done((s32[16,14]{1,0:T(8,128)S(1)}, s32[16,14]{1,0:T(8,128)}, u32[]{:S(2)}) %copy-start) | copy-done | bytes 920
  2.0 53.8 %shard_map.59 = bf16[4,32,2048]{2,1,0:T(8,128)(2,1)S(1)} custom-call(s32[16,14]{1,0:T(8,128)S(1)} %copy-done, s32[16]{0:T(128)S(1)} %copy-done.1, bf16[3,32,2048]{2,1,0:T(8,128)(2,1)} %bitcast.8, bf16[32,2048]{1,0:T(8,128)(2,1)} %bitcast.9), custom_call_target="tpu_custom_call" | custom-call | tf_op jit(solution)/shard_map/pallas_call | solution.py:223
  55.8 0.7 %slice.6 = bf16[1,32,2048]{2,1,0:T(8,128)(2,1)} slice(bf16[4,32,2048]{2,1,0:T(8,128)(2,1)S(1)} %shard_map.59), slice={[0:1], [0:32], [0:2048]} | slice | bytes 262144 | tf_op jit(solution)/shard_map/slice | solution.py:245
  56.5 0.8 %slice_bitcast_fusion = bf16[1,32,3,2048]{3,1,2,0:T(8,128)(2,1)} fusion(bf16[4,32,2048]{2,1,0:T(8,128)(2,1)S(1)} %shard_map.59), kind=kLoop, calls=%fused_computation | loop fusion | bytes 786432 | tf_op jit(solution)/shard_map/broadcast_in_dim | solution.py:245
Async XLA Ops:
  0.6 0.7 %copy-start.1 = (s32[16]{0:T(128)S(1)}, s32[16]{0:T(128)}, u32[]{:S(2)}) copy-start(s32[16]{0:T(128)} %count_ref.1) | copy-start | bytes 196
  1.3 0.7 %copy-start = (s32[16,14]{1,0:T(8,128)S(1)}, s32[16,14]{1,0:T(8,128)}, u32[]{:S(2)}) copy-start(s32[16,14]{1,0:T(8,128)} %blocks_ref.1) | copy-start | bytes 2692

commit v3 on v2

--- a/solution.py
+++ b/solution.py
@@ -128,9 +128,9 @@
 
 
 def kernel(
-    blocks_ref, count_ref, x_hbm, g_hbm, r_out,
-    x_ref, g_ref, r_ref, kt_ref, vt_ref, s_ref, e_ref, dk_ref, dv_ref, words_ref,
-    send_x, send_g, send_r, recv_kv, recv_q, recv_g, recv_r,
+    blocks_hbm, count_hbm, x_hbm, g_hbm, r_out,
+    x_ref, g_ref, r_ref, kt_ref, vt_ref, s_ref, e_ref, dk_ref, dv_ref, words_ref, blocks_ref, count_ref,
+    send_x, send_g, send_r, recv_kv, recv_q, recv_g, recv_r, tables_sem,
 ):
     pipe, seq, y = lax.axis_index("pipe"), lax.axis_index("seq"), lax.axis_index("head")
     is_owner, section, head = owned_by(pipe, seq, y)
@@ -151,6 +151,9 @@
             for to_y in ys:
                 lanes = pl.ds(pl.multiple_of(to_x * (4 * HD) + to_y * HD, HD), HD)
                 yield lanes, (2 * z_lo + of % 2, to_seq, to_y)
+
+    for _, device in owners(pipe):
+        ring(device)
 
     @pl.when(is_owner)
     def _():
@@ -161,8 +164,6 @@
                     ring(((section + 1) % N_PIPE, to_seq, to_y))
                     ring(((section + 3) % N_PIPE, to_seq, to_y))
 
-    for _, device in owners(pipe):
-        ring(device)
     pl.semaphore_wait(barrier, 32 + 64 * is_owner.astype(jnp.int32))
 
     mine = pl.ds(pl.multiple_of(seq * BLK + y * ROWS, ROWS), ROWS)
@@ -186,6 +187,10 @@
     @pl.when(is_owner)
     def _():
         my_lanes = pl.ds(pl.multiple_of(head * HD, HD), HD)
+        for table_hbm, table_ref, k in ((blocks_hbm, blocks_ref, 0), (count_hbm, count_ref, 1)):
+            copy = pltpu.make_async_copy(table_hbm, table_ref, tables_sem.at[k])
+            copy.start()
+            copy.wait()
         kept_words(blocks_ref, count_ref, words_ref)
 
         def bias(b, j):
@@ -214,16 +219,14 @@
 
 
 def body(section_input, grad_input, strided_blocks, strided_count):
-    x = jnp.transpose(section_input[0], (1, 0, 2))
-    g = pltpu.with_memory_space_constraint(grad_input[0], pltpu.HBM)
-    x = pltpu.with_memory_space_constraint(x, pltpu.HBM)
+    operands = (strided_blocks, strided_count, jnp.transpose(section_input[0], (1, 0, 2)), grad_input[0])
+    operands = [pltpu.with_memory_space_constraint(operand, pltpu.HBM) for operand in operands]
     hbm = pl.BlockSpec(memory_space=pl.ANY)
-    smem = pl.BlockSpec(memory_space=pltpu.SMEM)
     width = HEADS * HD
     result = pl.pallas_call(
         kernel,
         out_shape=jax.ShapeDtypeStruct((4, ROWS, width), BF16),
-        in_specs=[smem, smem, hbm, hbm],
+        in_specs=[hbm] * 4,
         out_specs=hbm,
         scratch_shapes=[
             pltpu.VMEM((3, SEQ, HD), BF16),
@@ -236,12 +239,15 @@
             pltpu.VMEM((SEQ, HD), F32),
             pltpu.VMEM((SEQ, HD), F32),
             pltpu.SMEM((NB,), jnp.int32),
+            pltpu.SMEM((NB, SMAX), jnp.int32),
+            pltpu.SMEM((NB,), jnp.int32),
         ]
-        + [pltpu.SemaphoreType.DMA] * 7,
+        + [pltpu.SemaphoreType.DMA] * 7
+        + [pltpu.SemaphoreType.DMA((2,))],
         compiler_params=pltpu.CompilerParams(
             collective_id=0, has_side_effects=True, vmem_limit_bytes=VMEM_LIMIT
         ),
-    )(strided_blocks, strided_count, x, g)
+    )(*operands)
     return result[:1], jnp.transpose(result[1:], (1, 0, 2))[None]
 
 

time: 57.4 us -> 55.9 us (0.974)
  local copies, waits for them, and re-layouts: 2.78 us -> 1.44 us
    unnamed x4 -> x0, local copies, waits for them, and re-layouts: 1.34 us -> none
where the time goes in v3:
time: 55.9 us; the launch traced here: 55.8 us
  Pallas kernels  53.7 us (96%)
  local copies, waits for them, and re-layouts  1.44 us (3%)
  between operations  0.64 us (1%)
    pallas_call x1, Pallas kernels, body(): pl.pallas_call(kernel, out_shape=jax.ShapeDtypeStruct((4, ROWS, width), B...  53.7 us

profile of v3, /device:TPU:1, one launch (start us, length us, event | category | flops | bytes accessed | tf_op | source)
XLA Modules:
  0.0 55.8 jit_solution(14480338420310838837)
XLA Ops:
  0.6 53.7 %shard_map.59 = bf16[4,32,2048]{2,1,0:T(8,128)(2,1)S(1)} custom-call(s32[16,14]{1,0:T(8,128)} %blocks_hbm.1, s32[16]{0:T(128)} %count_hbm.1, bf16[3,32,2048]{2,1,0:T(8,128)(2,1)} %bitcast.8, bf16[32,2048]{1,0:T(8,128)(2,1)} %bitcast.9), custom_call_target="tpu_custom_call" | custom-call | tf_op jit(solution)/shard_map/pallas_call | solution.py:226
  54.3 0.7 %slice.6 = bf16[1,32,2048]{2,1,0:T(8,128)(2,1)} slice(bf16[4,32,2048]{2,1,0:T(8,128)(2,1)S(1)} %shard_map.59), slice={[0:1], [0:32], [0:2048]} | slice | bytes 262144 | tf_op jit(solution)/shard_map/slice | solution.py:251
  55.0 0.8 %slice_bitcast_fusion = bf16[1,32,3,2048]{3,1,2,0:T(8,128)(2,1)} fusion(bf16[4,32,2048]{2,1,0:T(8,128)(2,1)S(1)} %shard_map.59), kind=kLoop, calls=%fused_computation | loop fusion | bytes 786432 | tf_op jit(solution)/shard_map/broadcast_in_dim | solution.py:251

commit v4 on v3

--- a/solution.py
+++ b/solution.py
@@ -146,9 +146,9 @@
 
     def owners(of):
         z_lo, shift = 1 - of // 2, (of % 2) * 2 + of // 2
-        for to_x in xs:
-            to_seq = to_x * 4 + (to_x + shift) % 4
-            for to_y in ys:
+        for to_y in ys:
+            for to_x in xs:
+                to_seq = to_x * 4 + (to_x + shift) % 4
                 lanes = pl.ds(pl.multiple_of(to_x * (4 * HD) + to_y * HD, HD), HD)
                 yield lanes, (2 * z_lo + of % 2, to_seq, to_y)
 

time: 55.9 us -> 56 us (level)
  no operation moved by 1% of the time
where the time goes in v4:
time: 56 us; the launch traced here: 55.9 us
  Pallas kernels  53.8 us (96%)
  local copies, waits for them, and re-layouts  1.44 us (3%)
  between operations  0.64 us (1%)
    pallas_call x1, Pallas kernels, body(): pl.pallas_call(kernel, out_shape=jax.ShapeDtypeStruct((4, ROWS, width), B...  53.8 us

profile of v4, /device:TPU:1, one launch (start us, length us, event | category | flops | bytes accessed | tf_op | source)
XLA Modules:
  0.0 55.9 jit_solution(15863616859070407116)
XLA Ops:
  0.6 53.8 %shard_map.59 = bf16[4,32,2048]{2,1,0:T(8,128)(2,1)S(1)} custom-call(s32[16,14]{1,0:T(8,128)} %blocks_hbm.1, s32[16]{0:T(128)} %count_hbm.1, bf16[3,32,2048]{2,1,0:T(8,128)(2,1)} %bitcast.8, bf16[32,2048]{1,0:T(8,128)(2,1)} %bitcast.9), custom_call_target="tpu_custom_call" | custom-call | tf_op jit(solution)/shard_map/pallas_call | solution.py:226
  54.4 0.7 %slice.6 = bf16[1,32,2048]{2,1,0:T(8,128)(2,1)} slice(bf16[4,32,2048]{2,1,0:T(8,128)(2,1)S(1)} %shard_map.59), slice={[0:1], [0:32], [0:2048]} | slice | bytes 262144 | tf_op jit(solution)/shard_map/slice | solution.py:251
  55.1 0.8 %slice_bitcast_fusion = bf16[1,32,3,2048]{3,1,2,0:T(8,128)(2,1)} fusion(bf16[4,32,2048]{2,1,0:T(8,128)(2,1)S(1)} %shard_map.59), kind=kLoop, calls=%fused_computation | loop fusion | bytes 786432 | tf_op jit(solution)/shard_map/broadcast_in_dim | solution.py:251

commit v5 on v3

--- a/solution.py
+++ b/solution.py
@@ -36,18 +36,19 @@
     return lax.dot_general(a, b, (((1,), (0,)), ((), ())), preferred_element_type=F32)
 
 
-def owner_of(section, head):
-    x, y = head // 4, head % 4
-    z_lo = 1 - section // 2
-    z_hi = (x + (section % 2) * 2 + section // 2) % 4
+def place_of(section):
+    return section + 0
+
+
+def owner_of(section, x, y):
+    z_lo, z_hi = (x + y) % 2, (x + place_of(section)) % 4
     return (2 * z_lo + section % 2, x * 4 + z_hi, y)
 
 
 def owned_by(pipe, seq, y):
     x, z_hi = seq // 4, seq % 4
-    half = 1 - pipe // 2
-    section = 2 * half + pipe % 2
-    is_owner = z_hi == (x + (pipe % 2) * 2 + half) % 4
+    section = place_of((z_hi + 4 - x) % 4)
+    is_owner = (section % 2 == pipe % 2) & ((x + y) % 2 == pipe // 2)
     return is_owner, section, x * 4 + y
 
 
@@ -145,15 +146,20 @@
         pl.semaphore_signal(barrier, inc=1, device_id=device, device_id_type=MESH)
 
     def owners(of):
-        z_lo, shift = 1 - of // 2, (of % 2) * 2 + of // 2
         for to_x in xs:
-            to_seq = to_x * 4 + (to_x + shift) % 4
             for to_y in ys:
                 lanes = pl.ds(pl.multiple_of(to_x * (4 * HD) + to_y * HD, HD), HD)
-                yield lanes, (2 * z_lo + of % 2, to_seq, to_y)
-
-    for _, device in owners(pipe):
+                yield lanes, owner_of(of, to_x, to_y)
+
+    owner = is_owner.astype(jnp.int32)
+    own = owner * (section == pipe).astype(jnp.int32)
+    *others, (_, last) = owners(pipe)
+    for _, device in others:
         ring(device)
+
+    @pl.when(own == 0)
+    def _():
+        ring(last)
 
     @pl.when(is_owner)
     def _():
@@ -164,7 +170,7 @@
                     ring(((section + 1) % N_PIPE, to_seq, to_y))
                     ring(((section + 3) % N_PIPE, to_seq, to_y))
 
-    pl.semaphore_wait(barrier, 32 + 64 * is_owner.astype(jnp.int32))
+    pl.semaphore_wait(barrier, 32 + 64 * owner - own)
 
     mine = pl.ds(pl.multiple_of(seq * BLK + y * ROWS, ROWS), ROWS)
 
@@ -207,11 +213,27 @@
             for to_y in ys:
                 for to_seq in (2 * b, 2 * b + 1):
                     rows = pl.ds(pl.multiple_of(to_seq * BLK + to_y * ROWS, ROWS), ROWS)
-                    pass_on(
-                        r_ref.at[:, rows, :], r_out.at[:, :, my_lanes], send_r, recv_r,
-                        (section, to_seq, to_y),
-                    )
-        wait_all(r_ref, send_r)
+                    piece, place = r_ref.at[:, rows, :], r_out.at[:, :, my_lanes]
+                    if to_y is not ys[-1]:
+                        pass_on(piece, place, send_r, recv_r, (section, to_seq, to_y))
+                        continue
+                    here = own * (seq == to_seq).astype(jnp.int32)
+
+                    @pl.when(here == 0)
+                    def _():
+                        pass_on(piece, place, send_r, recv_r, (section, to_seq, to_y))
+
+                    @pl.when(here == 1)
+                    def _():
+                        pltpu.make_async_copy(piece, place, recv_r).start()
+
+        @pl.when(own == 0)
+        def _():
+            wait_all(r_ref, send_r)
+
+        @pl.when(own == 1)
+        def _():
+            wait_all(r_ref.at[:, pl.ds(ROWS, SEQ - ROWS), :], send_r)
 
     wait_all(x_hbm, send_x)
     wait_all(g_hbm, send_g)

time: 55.9 us -> 55.7 us (level)
  no operation moved by 1% of the time
where the time goes in v5:
time: 55.7 us; the launch traced here: 55.6 us
  Pallas kernels  53.5 us (96%)
  local copies, waits for them, and re-layouts  1.44 us (3%)
  between operations  0.64 us (1%)
    pallas_call x1, Pallas kernels, body(): pl.pallas_call(kernel, out_shape=jax.ShapeDtypeStruct((4, ROWS, width), B...  53.5 us

profile of v5, /device:TPU:1, one launch (start us, length us, event | category | flops | bytes accessed | tf_op | source)
XLA Modules:
  0.0 55.6 jit_solution(12517160949745982975)
XLA Ops:
  0.6 53.5 %shard_map.59 = bf16[4,32,2048]{2,1,0:T(8,128)(2,1)S(1)} custom-call(s32[16,14]{1,0:T(8,128)} %blocks_hbm.1, s32[16]{0:T(128)} %count_hbm.1, bf16[3,32,2048]{2,1,0:T(8,128)(2,1)} %bitcast.8, bf16[32,2048]{1,0:T(8,128)(2,1)} %bitcast.9), custom_call_target="tpu_custom_call" | custom-call | tf_op jit(solution)/shard_map/pallas_call | solution.py:248
  54.1 0.7 %slice.6 = bf16[1,32,2048]{2,1,0:T(8,128)(2,1)} slice(bf16[4,32,2048]{2,1,0:T(8,128)(2,1)S(1)} %shard_map.59), slice={[0:1], [0:32], [0:2048]} | slice | bytes 262144 | tf_op jit(solution)/shard_map/slice | solution.py:273
  54.8 0.8 %slice_bitcast_fusion = bf16[1,32,3,2048]{3,1,2,0:T(8,128)(2,1)} fusion(bf16[4,32,2048]{2,1,0:T(8,128)(2,1)S(1)} %shard_map.59), kind=kLoop, calls=%fused_computation | loop fusion | bytes 786432 | tf_op jit(solution)/shard_map/broadcast_in_dim | solution.py:273
